TPU v7x, 32 devices: a whole 2x2x4 slice. The times are simulated.
32 devices in a mesh: strip: 2 (over y), col: 4 (over z), row: 4 (over x, core).
Axes of the slice: x: 2, y: 2, z: 4, core: 2. Of those that a mesh axis runs over, the one named last changes fastest.
Arguments:
- left_features: bfloat16 [64, 2048, 128], P(('strip', 'row'), 'col'), parts along dimension 0, may hold values from -6 to 6
- right_features: bfloat16 [64, 2048, 128], P(('strip', 'row'), 'col'), parts along dimension 0, may hold values from -6 to 6
- conv_first: bfloat16 [3, 3, 256, 256], replicated, may hold values from -0.125 to 0.125
- conv_second: bfloat16 [3, 3, 256, 256], replicated, may hold values from -0.125 to 0.125
Outputs:
- cost_field: bfloat16 [64, 2048, 256], P(('strip', 'row'), 'col'), parts along dimension 0
There are 2 independent parts, one for each index of `strip`. A program takes and returns all parts, laid end to end along the dimension named above; an argument that names none is the same for every part. Nothing has to cross between parts.
All inputs are finite; a program needn't handle non-finite values.
Results may differ from a plain program's by a relative error of at most 0.0058.
Values may be sent and summed in bfloat16 or wider, within the bound.
A program may use at most 128 MiB of HBM per device.

v0:
```python
import jax
import jax.numpy as jnp
from jax import lax
from jax.sharding import PartitionSpec as P


def passed_along(value, axis, steps):
    count = lax.axis_size(axis)
    initial, last = (max(0, -steps), min(count, count - steps))
    return lax.ppermute(value, axis, [(source, source + steps) for source in range(initial, last)])


def extended_2(block, sides, width):
    for axis, dim in sides:
        count = lax.axis_size(axis)
        forward = [(i, i + 1) for i in range(count - 1)]
        backward = [(target, source) for source, target in forward]
        low = lax.ppermute(
            lax.slice_in_dim(block, block.shape[dim] - width, None, axis=dim), axis, forward
        )
        high = lax.ppermute(lax.slice_in_dim(block, 0, width, axis=dim), axis, backward)
        block = jnp.concatenate([low, block, high], axis=dim)
    return block


def correlate(left_part, extended, disparities):
    row_count, col_count, chan_count = left_part.shape
    block_count = col_count // disparities
    left_blocks = left_part.reshape(row_count, block_count, disparities, chan_count)
    right_blocks = extended.reshape(row_count, block_count + 1, disparities, chan_count)
    windows = jnp.concatenate((right_blocks[:, :-1], right_blocks[:, 1:]), axis=2)
    scores = jnp.einsum("rjwc,rjvc->rjwv", left_blocks, windows, preferred_element_type=jnp.float32)
    scores = scores * (1.0 / jnp.sqrt(jnp.float32(chan_count)))
    flat_scores = scores.reshape(row_count, block_count, disparities * 2 * disparities)
    flat_scores = jnp.pad(flat_scores, ((0, 0), (0, 0), (0, disparities)))
    skewed = flat_scores.reshape(row_count, block_count, disparities, 2 * disparities + 1)
    banded = skewed[..., 1 : disparities + 1][..., ::-1]
    return banded.reshape(row_count, col_count, disparities).astype(jnp.bfloat16)


def convolve_valid(padded, kernel):
    result = lax.conv_general_dilated(
        padded[None],
        kernel,
        (1, 1),
        "VALID",
        dimension_numbers=("NHWC", "HWIO", "NHWC"),
        preferred_element_type=jnp.float32,
    )
    return result[0]


def local(left_features, right_features, conv_first, conv_second):
    disparities = conv_first.shape[2]
    earlier = passed_along(right_features[:, -disparities:], "col", 1)
    extended = jnp.concatenate((earlier, right_features), axis=1)
    volume = correlate(left_features, extended, disparities)
    padded = extended_2(volume, (("col", 1), ("row", 0)), 1)
    hidden = jax.nn.relu(convolve_valid(padded, conv_first)).astype(jnp.bfloat16)
    padded_hidden = extended_2(hidden, (("col", 1), ("row", 0)), 1)
    result = jax.nn.relu(convolve_valid(padded_hidden, conv_second)).astype(jnp.bfloat16)
    return result


def solution(mesh):
    in_specs = (P(("strip", "row"), "col", None), P(("strip", "row"), "col", None), P(), P())
    out_specs = P(("strip", "row"), "col", None)
    return jax.shard_map(local, mesh=mesh, in_specs=in_specs, out_specs=out_specs, check_vma=False)
```

profile of v0, /device:TPU:1, one launch (start us, length us, event | category | flops | bytes accessed | tf_op | source)
XLA Modules:
  0.0 145.7 jit_solution(355283094916841175)
XLA Ops:
  0.0 0.0 copy-start
  0.0 1.2 slice.36
  1.2 4.1 %collective-permute-start = (bf16[8,256,128]{2,1,0:T(8,128)(2,1)S(1)}, bf16[8,256,128]{2,1,0:T(8,128)(2,1)S(1)}, u32[]{:S(2)}, u32[]{:S(2)}) collective-permute-start(bf16[8,256,128]{2,1,0:T(8,128)(2,1)S(1)} %slice.36), channel_id=1, source_target_pairs={{0,4},{4,8},{8,12},{1,5},{5,9},{9,13},{2,6},{6,10},{10,14},{3,7},{... | collective-permute-start | bytes 1572872 | tf_op jit(solution)/shard_map/ppermute | solution.py:10
  5.2 10.6 %collective-permute-done = bf16[8,256,128]{2,1,0:T(8,128)(2,1)S(1)} collective-permute-done((bf16[8,256,128]{2,1,0:T(8,128)(2,1)S(1)}, bf16[8,256,128]{2,1,0:T(8,128)(2,1)S(1)}, u32[]{:S(2)}, u32[]{:S(2)}) %collective-permute-start) | collective-permute-done | bytes 524320 | tf_op jit(solution)/shard_map/ppermute | solution.py:10
  15.8 1.3 pad_maximum_fusion
  17.1 0.0 copy-start.3
  17.1 0.4 fusion.34
  17.5 0.8 copy-done.3
  18.4 3.2 %multiply_bitcast_fusion = bf16[8,2,256,512]{2,3,1,0:T(8,128)(2,1)} fusion(bf16[8,2,256,128]{3,2,1,0:T(8,128)(2,1)S(1)} %bitcast.46, bf16[8,2,256,128]{3,2,1,0:T(8,128)(2,1)S(1)} %get-tuple-element.14, bf16[8,2,256,128]{3,2,1,0:T(8,128)(2,1)S(1)} %get-tuple-element.13), kind=kOutput, calls=%fused_computation | convolution fusion | flops 545259520 | bytes 7340032 | tf_op jit(solution)/shard_map/rjwc,rjvc->rjwv/dot_general | solution.py:32
  21.6 6.2 %copy.24 = bf16[8,2,256,512]{3,2,0,1:T(8,128)(2,1)} copy(bf16[8,2,256,512]{2,3,1,0:T(8,128)(2,1)} %multiply_bitcast_fusion) | data formatting | bytes 8388608 | tf_op jit(solution)/shard_map/mul | solution.py:33
  27.8 4.9 %reshape.22 = bf16[8,2,131072]{2,0,1:T(8,128)(2,1)} reshape(bf16[8,2,256,512]{3,2,0,1:T(8,128)(2,1)} %copy.24) | data formatting | bytes 8388608 | tf_op jit(solution)/shard_map/reshape | solution.py:34
  32.7 3.7 %pad.4 = bf16[8,2,131328]{2,0,1:T(8,128)(2,1)} pad(bf16[8,2,131072]{2,0,1:T(8,128)(2,1)} %reshape.22, bf16[]{:T(256)} %constant.10), padding=0_0x0_0x0_256 | pad | bytes 8396802 | tf_op jit(solution)/shard_map/jit(_pad)/pad | solution.py:35
  36.4 13.3 %reshape.23 = bf16[8,2,256,513]{3,2,0,1:T(8,128)(2,1)} reshape(bf16[8,2,131328]{2,0,1:T(8,128)(2,1)} %pad.4) | data formatting | bytes 8404992 | tf_op jit(solution)/shard_map/reshape | solution.py:36
  49.7 2.9 %slice.54 = bf16[8,2,256,256]{3,2,0,1:T(8,128)(2,1)S(1)} slice(bf16[8,2,256,513]{3,2,0,1:T(8,128)(2,1)} %reshape.23), slice={[0:8], [0:2], [0:256], [1:257]} | slice | bytes 4194304 | tf_op jit(solution)/shard_map/slice | solution.py:37
  52.7 22.5 %rev.3 = bf16[8,2,256,256]{3,2,0,1:T(8,128)(2,1)} reverse(bf16[8,2,256,256]{3,2,0,1:T(8,128)(2,1)S(1)} %slice.54), dimensions={3} | reverse | bytes 4194304 | tf_op jit(solution)/shard_map/rev | solution.py:37
  75.1 1.7 %copy.25 = bf16[8,2,256,256]{3,2,1,0:T(8,128)(2,1)S(1)} copy(bf16[8,2,256,256]{3,2,0,1:T(8,128)(2,1)} %rev.3) | data formatting | bytes 4194304 | tf_op jit(solution)/shard_map/convert_element_type | solution.py:38
  76.9 4.1 %collective-permute-start.1 = (bf16[8,1,256]{2,1,0:T(2,128)(2,1)S(1)}, bf16[8,1,256]{2,1,0:T(2,128)(2,1)S(1)}, u32[]{:S(2)}, u32[]{:S(2)}) collective-permute-start(bf16[8,1,256]{2,1,0:T(2,128)(2,1)S(1)} %get-tuple-element.11), channel_id=1, source_target_pairs={{0,4},{4,8},{8,12},{1,5},{5,9},{9,13},{2,6},{6,10},{10,14},{3,7},{... | collective-permute-start | bytes 12296 | tf_op jit(solution)/shard_map/ppermute | solution.py:18
  81.0 1.3 collective-permute-start.2
  82.3 0.0 collective-permute-done.1
  82.3 3.1 %collective-permute-done.2 = bf16[8,1,256]{2,1,0:T(2,128)(2,1)S(1)} collective-permute-done((bf16[8,1,256]{2,1,0:T(2,128)(2,1)S(1)}, bf16[8,1,256]{2,1,0:T(2,128)(2,1)S(1)}, u32[]{:S(2)}, u32[]{:S(2)}) %collective-permute-start.2) | collective-permute-done | bytes 4128 | tf_op jit(solution)/shard_map/ppermute | solution.py:21
  85.4 0.1 pad_maximum_fusion.6
  85.5 6.0 %collective-permute-start.3 = (bf16[1,514,256]{2,1,0:T(8,128)(2,1)S(1)}, bf16[1,514,256]{2,1,0:T(8,128)(2,1)S(1)}, u32[]{:S(2)}, u32[]{:S(2)}) collective-permute-start(bf16[1,514,256]{2,1,0:T(8,128)(2,1)S(1)} %get-tuple-element.5), channel_id=1, source_target_pairs={{0,1},{1,2},{2,3},{4,5},{5,6},{6,7},{8,9},{9,10},{10,11},{12,13},{... | collective-permute-start | bytes 789512 | tf_op jit(solution)/shard_map/ppermute | solution.py:18
  91.5 2.1 %collective-permute-start.4 = (bf16[1,514,256]{2,1,0:T(8,128)(2,1)S(1)}, bf16[1,514,256]{2,1,0:T(8,128)(2,1)S(1)}, u32[]{:S(2)}, u32[]{:S(2)}) collective-permute-start(bf16[1,514,256]{2,1,0:T(8,128)(2,1)S(1)} %get-tuple-element.6), channel_id=1, source_target_pairs={{1,0},{2,1},{3,2},{5,4},{6,5},{7,6},{9,8},{10,9},{11,10},{13,12},{... | collective-permute-start | bytes 789512 | tf_op jit(solution)/shard_map/ppermute | solution.py:21
  93.6 1.2 collective-permute-done.3
  94.9 4.4 %collective-permute-done.4 = bf16[1,514,256]{2,1,0:T(8,128)(2,1)S(1)} collective-permute-done((bf16[1,514,256]{2,1,0:T(8,128)(2,1)S(1)}, bf16[1,514,256]{2,1,0:T(8,128)(2,1)S(1)}, u32[]{:S(2)}, u32[]{:S(2)}) %collective-permute-start.4) | collective-permute-done | bytes 263200 | tf_op jit(solution)/shard_map/ppermute | solution.py:21
  99.2 0.8 maximum_bitcast_fusion.1
  100.0 1.7 %pad.5 = bf16[10,1,520,256]{3,2,0,1:T(8,128)(2,1)} pad(bf16[10,1,514,256]{3,2,0,1:T(8,128)(2,1)S(1)} %maximum_bitcast_fusion.1, bf16[]{:T(256)} %constant.10), padding=0_0x0_0x0_6x0_0 | pad | bytes 5294082 | tf_op jit(solution)/shard_map/broadcast_in_dim | solution.py:43
  101.8 5.1 %reshape.26 = bf16[10,1,8,65,256]{4,3,2,0,1:T(8,128)(2,1)} reshape(bf16[10,1,520,256]{3,2,0,1:T(8,128)(2,1)} %pad.5) | data formatting | bytes 5324800 | tf_op jit(solution)/shard_map/conv_general_dilated | solution.py:42
  106.9 0.0 copy-start.4
  106.9 2.4 %copy.27 = bf16[10,1,8,65,256]{4,2,3,0,1:T(8,128)(2,1)S(1)} copy(bf16[10,1,8,65,256]{4,3,2,0,1:T(8,128)(2,1)} %reshape.26) | data formatting | bytes 5324800 | tf_op jit(solution)/shard_map/conv_general_dilated | solution.py:42
  109.3 0.0 copy-done
  109.3 0.0 copy-done.4
  109.3 5.4 %maximum_convert_fusion.1 = bf16[8,8,65,256]{3,1,2,0:T(8,128)(2,1)S(1)} fusion(pred[8,65]{0,1:T(8,128)(4,1)S(1)} %copy-done.4, bf16[3,3,256,256]{3,2,1,0:T(8,128)(2,1)S(1)} %copy-done, bf16[10,1,7,2,256]{4,2,3,0,1:T(8,128)(2,1)S(1)} %slice.57, bf16[10,1,8,65,256]{4,2,3,0,1:T(8,128)(2,1)S(1)} %copy.27), kind=kOutput, calls=%fused_computation.5 | convolution fusion | flops 4918763520 | bytes 6044168 | tf_op jit(solution)/shard_map/conv_general_dilated | solution.py:42
  114.7 0.4 copy.28
  115.2 0.1 slice_bitcast_fusion.1
  115.3 3.2 %collective-permute-start.5 = (bf16[8,1,256]{2,0,1:T(8,128)(2,1)S(1)}, bf16[8,1,256]{2,0,1:T(8,128)(2,1)S(1)}, u32[]{:S(2)}, u32[]{:S(2)}) collective-permute-start(bf16[8,1,256]{2,0,1:T(8,128)(2,1)S(1)} %get-tuple-element.9), channel_id=1, source_target_pairs={{0,4},{4,8},{8,12},{1,5},{5,9},{9,13},{2,6},{6,10},{10,14},{3,7},{... | collective-permute-start | bytes 12296 | tf_op jit(solution)/shard_map/ppermute | solution.py:18
  118.5 1.3 collective-permute-start.6
  119.8 0.0 collective-permute-done.5
  119.8 3.0 %collective-permute-done.6 = bf16[8,1,256]{2,0,1:T(8,128)(2,1)S(1)} collective-permute-done((bf16[8,1,256]{2,0,1:T(8,128)(2,1)S(1)}, bf16[8,1,256]{2,0,1:T(8,128)(2,1)S(1)}, u32[]{:S(2)}, u32[]{:S(2)}) %collective-permute-start.6) | collective-permute-done | bytes 4128 | tf_op jit(solution)/shard_map/ppermute | solution.py:21
  122.9 0.8 pad_maximum_fusion.3
  123.8 1.9 %collective-permute-start.8 = (bf16[1,514,256]{2,1,0:T(8,128)(2,1)S(1)}, bf16[1,514,256]{2,1,0:T(8,128)(2,1)S(1)}, u32[]{:S(2)}, u32[]{:S(2)}) collective-permute-start(bf16[1,514,256]{2,1,0:T(8,128)(2,1)S(1)} %copy.30), channel_id=1, source_target_pairs={{1,0},{2,1},{3,2},{5,4},{6,5},{7,6},{9,8},{10,9},{11,10},{13,12},{... | collective-permute-start | bytes 789512 | tf_op jit(solution)/shard_map/ppermute | solution.py:21
  125.8 3.9 %collective-permute-start.7 = (bf16[1,514,256]{2,1,0:T(8,128)(2,1)S(1)}, bf16[1,514,256]{2,1,0:T(8,128)(2,1)S(1)}, u32[]{:S(2)}, u32[]{:S(2)}) collective-permute-start(bf16[1,514,256]{2,1,0:T(8,128)(2,1)S(1)} %copy.29), channel_id=1, source_target_pairs={{0,1},{1,2},{2,3},{4,5},{5,6},{6,7},{8,9},{9,10},{10,11},{12,13},{... | collective-permute-start | bytes 789512 | tf_op jit(solution)/shard_map/ppermute | solution.py:18
  129.6 1.9 %collective-permute-done.8 = bf16[1,514,256]{2,1,0:T(8,128)(2,1)S(1)} collective-permute-done((bf16[1,514,256]{2,1,0:T(8,128)(2,1)S(1)}, bf16[1,514,256]{2,1,0:T(8,128)(2,1)S(1)}, u32[]{:S(2)}, u32[]{:S(2)}) %collective-permute-start.8) | collective-permute-done | bytes 263200 | tf_op jit(solution)/shard_map/ppermute | solution.py:21
  131.5 0.4 copy.32
  131.9 0.8 collective-permute-done.7
  132.7 0.4 copy.31
  133.2 3.0 %maximum_bitcast_fusion = bf16[10,1,514,256]{3,0,2,1:T(8,128)(2,1)S(1)} fusion(bf16[1,514,256]{2,0,1:T(2,128)(2,1)S(1)} %copy.32, bf16[8,1,256]{2,0,1:T(8,128)(2,1)S(1)} %collective-permute-done.6, bf16[8,512,256]{2,0,1:T(8,128)(2,1)S(1)} %slice_bitcast_fusion.1, bf16[8,1,256]{2,0,1:T(8,128)(2,1)S(1)} %collective-permute-done.5, bf16[1,514,256]{2,0,1:T(2,128)(2,1)S(1)} %copy.31), kind=kLoop, calls=%fused_computation.6 | loop fusion | flops 13158400 | bytes 5263360 | tf_op jit(solution)/shard_map/broadcast_in_dim | solution.py:43
  136.2 0.5 pad.7
  136.7 0.0 copy-start.2
  136.7 1.0 copy.35
  137.7 0.2 copy-done.2
  138.0 5.4 %maximum_convert_fusion = bf16[8,8,65,256]{3,1,2,0:T(8,128)(2,1)S(1)} fusion(pred[8,65]{0,1:T(8,128)(4,1)S(1)} %copy-done.4, bf16[3,3,256,256]{3,2,1,0:T(8,128)(2,1)S(1)} %copy-done.2, bf16[10,1,7,2,256]{4,2,3,0,1:T(8,128)(2,1)S(1)} %slice.61, bf16[10,1,8,65,256]{4,2,3,0,1:T(8,128)(2,1)S(1)} %copy.35), kind=kOutput, calls=%fused_computation.4 | convolution fusion | flops 4918763520 | bytes 6044168 | tf_op jit(solution)/shard_map/conv_general_dilated | solution.py:42
  143.4 0.4 copy.36
  143.8 0.0 copy-start.1
  143.8 0.1 slice_bitcast_fusion
  144.0 1.7 %copy.37 = bf16[8,512,256]{2,1,0:T(8,128)(2,1)} copy(bf16[8,512,256]{2,0,1:T(8,128)(2,1)S(1)} %slice_bitcast_fusion) | data formatting | bytes 4194304 | tf_op jit(solution)/shard_map/convert_element_type | solution.py:61
  145.7 0.0 copy-done.1
  (6 shorter events, 0.1 us)
Async XLA Ops:
  0.0 109.3 %copy-start = (bf16[3,3,256,256]{3,2,1,0:T(8,128)(2,1)S(1)}, bf16[3,3,256,256]{3,2,1,0:T(8,128)(2,1)}, u32[]{:S(2)}) copy-start(bf16[3,3,256,256]{3,2,1,0:T(8,128)(2,1)} %param.6) | copy-start | bytes 3538948
  1.2 14.6 %collective-permute-start = (bf16[8,256,128]{2,1,0:T(8,128)(2,1)S(1)}, bf16[8,256,128]{2,1,0:T(8,128)(2,1)S(1)}, u32[]{:S(2)}, u32[]{:S(2)}) collective-permute-start(bf16[8,256,128]{2,1,0:T(8,128)(2,1)S(1)} %slice.36), channel_id=1, source_target_pairs={{0,4},{4,8},{8,12},{1,5},{5,9},{9,13},{2,6},{6,10},{10,14},{3,7},{... | collective-permute-start | bytes 1572872 | tf_op jit(solution)/shard_map/ppermute | solution.py:10
  17.1 1.2 copy-start.3
  76.9 5.4 %collective-permute-start.1 = (bf16[8,1,256]{2,1,0:T(2,128)(2,1)S(1)}, bf16[8,1,256]{2,1,0:T(2,128)(2,1)S(1)}, u32[]{:S(2)}, u32[]{:S(2)}) collective-permute-start(bf16[8,1,256]{2,1,0:T(2,128)(2,1)S(1)} %get-tuple-element.11), channel_id=1, source_target_pairs={{0,4},{4,8},{8,12},{1,5},{5,9},{9,13},{2,6},{6,10},{10,14},{3,7},{... | collective-permute-start | bytes 12296 | tf_op jit(solution)/shard_map/ppermute | solution.py:18
  81.0 4.4 %collective-permute-start.2 = (bf16[8,1,256]{2,1,0:T(2,128)(2,1)S(1)}, bf16[8,1,256]{2,1,0:T(2,128)(2,1)S(1)}, u32[]{:S(2)}, u32[]{:S(2)}) collective-permute-start(bf16[8,1,256]{2,1,0:T(2,128)(2,1)S(1)} %get-tuple-element.12), channel_id=1, source_target_pairs={{4,0},{8,4},{12,8},{5,1},{9,5},{13,9},{6,2},{10,6},{14,10},{7,3},{... | collective-permute-start | bytes 12296 | tf_op jit(solution)/shard_map/ppermute | solution.py:21
  85.5 9.3 %collective-permute-start.3 = (bf16[1,514,256]{2,1,0:T(8,128)(2,1)S(1)}, bf16[1,514,256]{2,1,0:T(8,128)(2,1)S(1)}, u32[]{:S(2)}, u32[]{:S(2)}) collective-permute-start(bf16[1,514,256]{2,1,0:T(8,128)(2,1)S(1)} %get-tuple-element.5), channel_id=1, source_target_pairs={{0,1},{1,2},{2,3},{4,5},{5,6},{6,7},{8,9},{9,10},{10,11},{12,13},{... | collective-permute-start | bytes 789512 | tf_op jit(solution)/shard_map/ppermute | solution.py:18
  91.5 7.7 %collective-permute-start.4 = (bf16[1,514,256]{2,1,0:T(8,128)(2,1)S(1)}, bf16[1,514,256]{2,1,0:T(8,128)(2,1)S(1)}, u32[]{:S(2)}, u32[]{:S(2)}) collective-permute-start(bf16[1,514,256]{2,1,0:T(8,128)(2,1)S(1)} %get-tuple-element.6), channel_id=1, source_target_pairs={{1,0},{2,1},{3,2},{5,4},{6,5},{7,6},{9,8},{10,9},{11,10},{13,12},{... | collective-permute-start | bytes 789512 | tf_op jit(solution)/shard_map/ppermute | solution.py:21
  106.9 2.5 %copy-start.4 = (pred[8,65]{0,1:T(8,128)(4,1)S(1)}, pred[8,65]{0,1:T(8,128)(4,1)}, u32[]{:S(2)}) copy-start(pred[8,65]{0,1:T(8,128)(4,1)} %constant.18) | copy-start | bytes 1564
  115.3 4.5 %collective-permute-start.5 = (bf16[8,1,256]{2,0,1:T(8,128)(2,1)S(1)}, bf16[8,1,256]{2,0,1:T(8,128)(2,1)S(1)}, u32[]{:S(2)}, u32[]{:S(2)}) collective-permute-start(bf16[8,1,256]{2,0,1:T(8,128)(2,1)S(1)} %get-tuple-element.9), channel_id=1, source_target_pairs={{0,4},{4,8},{8,12},{1,5},{5,9},{9,13},{2,6},{6,10},{10,14},{3,7},{... | collective-permute-start | bytes 12296 | tf_op jit(solution)/shard_map/ppermute | solution.py:18
  118.5 4.4 %collective-permute-start.6 = (bf16[8,1,256]{2,0,1:T(8,128)(2,1)S(1)}, bf16[8,1,256]{2,0,1:T(8,128)(2,1)S(1)}, u32[]{:S(2)}, u32[]{:S(2)}) collective-permute-start(bf16[8,1,256]{2,0,1:T(8,128)(2,1)S(1)} %get-tuple-element.10), channel_id=1, source_target_pairs={{4,0},{8,4},{12,8},{5,1},{9,5},{13,9},{6,2},{10,6},{14,10},{7,3},{... | collective-permute-start | bytes 12296 | tf_op jit(solution)/shard_map/ppermute | solution.py:21
  123.8 7.7 %collective-permute-start.8 = (bf16[1,514,256]{2,1,0:T(8,128)(2,1)S(1)}, bf16[1,514,256]{2,1,0:T(8,128)(2,1)S(1)}, u32[]{:S(2)}, u32[]{:S(2)}) collective-permute-start(bf16[1,514,256]{2,1,0:T(8,128)(2,1)S(1)} %copy.30), channel_id=1, source_target_pairs={{1,0},{2,1},{3,2},{5,4},{6,5},{7,6},{9,8},{10,9},{11,10},{13,12},{... | collective-permute-start | bytes 789512 | tf_op jit(solution)/shard_map/ppermute | solution.py:21
  125.8 7.0 %collective-permute-start.7 = (bf16[1,514,256]{2,1,0:T(8,128)(2,1)S(1)}, bf16[1,514,256]{2,1,0:T(8,128)(2,1)S(1)}, u32[]{:S(2)}, u32[]{:S(2)}) collective-permute-start(bf16[1,514,256]{2,1,0:T(8,128)(2,1)S(1)} %copy.29), channel_id=1, source_target_pairs={{0,1},{1,2},{2,3},{4,5},{5,6},{6,7},{8,9},{9,10},{10,11},{12,13},{... | collective-permute-start | bytes 789512 | tf_op jit(solution)/shard_map/ppermute | solution.py:18
  136.7 1.3 copy-start.2
  143.8 1.9 %copy-start.1 = (bf16[3,3,256,256]{3,2,1,0:T(8,128)(2,1)S(1)}, bf16[3,3,256,256]{3,2,1,0:T(8,128)(2,1)}, u32[]{:S(2)}) copy-start(bf16[3,3,256,256]{3,2,1,0:T(8,128)(2,1)} %param.6) | copy-start | bytes 3538948
where the time goes:
time: 147 us; the launch traced here: 146 us
  local copies, waits for them, and re-layouts  72.5 us (49%)
  starting transfers between devices  27.8 us (19%)
  waiting for transfers between devices  25 us (17%)
  matrix products  14 us (10%)
  other arithmetic  6.12 us (4%)
    rev x1, local copies, waits for them, and re-layouts, correlate(): banded = skewed[..., 1:disparities + 1][..., ::-1]  22.5 us
    ppermute x4, starting transfers between devices, extended_2(): lax.ppermute(lax.slice_in_dim(block, block.shape[dim] - width, None, axis...  17.1 us
    reshape x1, local copies, waits for them, and re-layouts, correlate(): flat_scores.reshape(row_count, block_count, disparities, 2 * disparities...  13.3 us
    ppermute x4, waiting for transfers between devices, extended_2(): lax.ppermute(lax.slice_in_dim(block, 0, width, axis=dim), axis, backward)  12.4 us
    conv_general_dilated x2, matrix products, convolve_valid(): lax.conv_general_dilated(padded[None], kernel, (1, 1), 'VALID', dimension...  10.8 us
    ppermute x1, waiting for transfers between devices, passed_along(): lax.ppermute(value, axis, [(source, source + steps) for source in range(i...  10.6 us
    conv_general_dilated x5, local copies, waits for them, and re-layouts, convolve_valid(): lax.conv_general_dilated(padded[None], kernel, (1, 1), 'VALID', dimension...  8.56 us
    ppermute x4, starting transfers between devices, extended_2(): lax.ppermute(lax.slice_in_dim(block, 0, width, axis=dim), axis, backward)  6.61 us
  transfers between devices with their start and end apart: 9, of which 7 were waited for; matrix products, arithmetic and copies ran while one was open for 0% of the time, Pallas kernels for 0%

commit v1 on v0

v1 whole, which is shorter than its diff:
```python
import functools

import jax
import jax.numpy as jnp
from jax import lax
from jax.experimental import pallas as pl
from jax.experimental.pallas import tpu as pltpu
from jax.sharding import PartitionSpec as P

MESH = pl.DeviceIdType.MESH
F32 = jnp.float32
BF16 = jnp.bfloat16
G = 16
TILE = 112
LANES = 128


def kernel(
    ncol, nrow, left, right, w1_hbm, w2_hbm, out,
    rext, lext, rrev, vol3, hid3, w1, w2, obuf, lsem, osem, ssem, rsem,
):
    rows, width, chans = left.shape
    disp = w1_hbm.shape[0] // 9
    col = lax.axis_index("col")
    row = lax.axis_index("row")
    has_l, has_r = col > 0, col < ncol - 1
    has_u, has_d = row > 0, row < nrow - 1
    to_l, to_r = {"col": col - 1}, {"col": col + 1}
    to_u, to_d = {"row": row - 1}, {"row": row + 1}
    reach = disp + G
    tiles = vol_cols(width) // TILE
    span = rext.shape[1]
    window = TILE_WINDOW(disp)
    hcols = width + G

    rext[:, 0:reach] = jnp.zeros((rows + 4, reach, chans), BF16)
    rext[:, reach + width :] = jnp.zeros((rows + 4, span - reach - width, chans), BF16)
    lext[:, 0:G] = jnp.zeros((rows + 4, G, chans), BF16)
    lext[:, G + width :] = jnp.zeros((rows + 4, lext.shape[1] - G - width, chans), BF16)
    for ref, at in ((rext, reach), (lext, G)):
        ref[0:2, at : at + width] = jnp.zeros((2, width, chans), BF16)
        ref[rows + 2 :, at : at + width] = jnp.zeros((2, width, chans), BF16)

    own = [
        pltpu.make_async_copy(right, rext.at[2 : rows + 2, reach : reach + width], lsem.at[0]),
        pltpu.make_async_copy(left, lext.at[2 : rows + 2, G : G + width], lsem.at[1]),
        pltpu.make_async_copy(w1_hbm, w1, lsem.at[2]),
        pltpu.make_async_copy(w2_hbm, w2, lsem.at[3]),
    ]
    for copy in own:
        copy.start()

    barrier = pltpu.get_barrier_semaphore()
    for has, to in ((has_l, to_l), (has_r, to_r), (has_u, to_u), (has_d, to_d)):
        @pl.when(has)
        def _():
            pl.semaphore_signal(barrier, inc=1, device_id=to, device_id_type=MESH)
    peers = sum(has.astype(jnp.int32) for has in (has_l, has_r, has_u, has_d))
    pl.semaphore_wait(barrier, peers)

    counter = [0]

    def remote(src, dst, to):
        at = counter[0]
        counter[0] += 1
        return pltpu.make_async_remote_copy(
            src_ref=src, dst_ref=dst, send_sem=ssem.at[at], recv_sem=rsem.at[at],
            device_id=to, device_id_type=MESH,
        )

    tail = width - reach
    far = reach + width
    chunks = [(0, 2), (rows - 2, rows)]
    middle = rows // 2
    chunks += [(2, middle), (middle, rows - 2)]
    small_r = [remote(left.at[:, width - G : width], lext.at[2 : rows + 2, 0:G], to_r)]
    parts = [
        remote(right.at[a:b, tail:width], rext.at[2 + a : 2 + b, 0:reach], to_r)
        for a, b in chunks
    ]
    small_l = [
        remote(left.at[:, 0:G], lext.at[2 : rows + 2, G + width : 2 * G + width], to_l),
        remote(right.at[:, 0:G], rext.at[2 : rows + 2, far : far + G], to_l),
    ]
    down = [
        remote(right.at[rows - 2 : rows], rext.at[0:2, reach:far], to_d),
        remote(left.at[rows - 2 : rows], lext.at[0:2, G : G + width], to_d),
    ]
    up = [
        remote(right.at[0:2], rext.at[rows + 2 : rows + 4, reach:far], to_u),
        remote(left.at[0:2], lext.at[rows + 2 : rows + 4, G : G + width], to_u),
    ]

    def edges(source, target, to):
        s, t = slice(source, source + 2), slice(target, target + 2)
        return [
            remote(rext.at[s, 0:reach], rext.at[t, 0:reach], to),
            remote(rext.at[s, far : far + G], rext.at[t, far : far + G], to),
            remote(lext.at[s, 0:G], lext.at[t, 0:G], to),
            remote(lext.at[s, G + width : 2 * G + width], lext.at[t, G + width : 2 * G + width], to),
        ]

    up_edges = edges(2, rows + 2, to_u)
    down_edges = edges(rows, 0, to_d)

    def start(has, copies):
        @pl.when(has)
        def _():
            for copy in copies:
                copy.start()

    def recv(has, copies):
        @pl.when(has)
        def _():
            for copy in copies:
                copy.wait_recv()

    def sent(has, copies):
        @pl.when(has)
        def _():
            for copy in copies:
                copy.wait_send()

    start(has_r, small_r + parts)
    start(has_l, small_l)
    start(has_d, down)
    start(has_u, up)

    block = span // 4
    i = lax.broadcasted_iota(jnp.int32, (block, block), 0)
    j = lax.broadcasted_iota(jnp.int32, (block, block), 1)
    flip = jnp.where(i + j == block - 1, 1.0, 0.0).astype(BF16)
    scale = 1.0 / jnp.sqrt(F32(chans))

    def correlate(first, count):
        @pl.loop(first, first + count)
        def _(r):
            for q in range(4):
                piece = jnp.dot(
                    flip, rext[r, q * block : (q + 1) * block, :], preferred_element_type=F32
                )
                rrev[(3 - q) * block : (4 - q) * block, :] = piece.astype(BF16)
            for t in range(tiles):
                at = span - window - TILE * t
                scores = lax.dot_general(
                    lext[r, TILE * t : TILE * (t + 1), :],
                    rrev[at : at + window, :],
                    (((1,), (1,)), ((), ())),
                    preferred_element_type=F32,
                )
                turned = pltpu.roll(
                    scores, disp + 1, 1, stride=1, stride_axis=0
                )[:, :disp]
                value = (turned * scale).astype(BF16)
                for b in range(3):
                    vol3[r, TILE * t + 2 - b : TILE * (t + 1) + 2 - b, b * disp : (b + 1) * disp] = value

    def first_conv(first, count):
        @pl.loop(first, first + count)
        def _(g):
            x = jnp.concatenate([vol3[g + a, G : G + hcols, :] for a in range(3)], axis=1)
            acc = jnp.dot(x, w1[...], preferred_element_type=F32)
            j = lax.broadcasted_iota(jnp.int32, (hcols, 1), 0)
            at_row = row * rows + g - 1
            at_col = col * width + j - 1
            inside = (at_col >= 0) & (at_col < ncol * width) & (at_row >= 0) & (at_row < nrow * rows)
            value = jnp.where(inside, jnp.maximum(acc, 0.0), 0.0).astype(BF16)
            for b in range(3):
                hid3[g, G - b : G - b + hcols, b * disp : (b + 1) * disp] = value

    def out_copy(h):
        return pltpu.make_async_copy(obuf.at[h], out.at[h], osem.at[h])

    def second_conv(first, count):
        @pl.loop(first, first + count)
        def _(h):
            x = jnp.concatenate([hid3[h + a, G : G + width, :] for a in range(3)], axis=1)
            acc = jnp.dot(x, w2[...], preferred_element_type=F32)
            obuf[h] = jnp.maximum(acc, 0.0).astype(BF16)
            out_copy(h).start()

    own[0].wait()
    own[1].wait()
    recv(has_l, small_r)
    recv(has_r, small_l)
    recv(has_l, [parts[0]])
    start(has_u, up_edges)
    correlate(2, 2)
    recv(has_l, [parts[1]])
    start(has_d, down_edges)
    correlate(rows, 2)
    recv(has_d, up + up_edges)
    correlate(rows + 2, 2)
    recv(has_l, [parts[2]])
    correlate(4, middle - 2)
    own[2].wait()
    own[3].wait()
    recv(has_u, down + down_edges)
    correlate(0, 2)
    first_conv(0, middle)
    second_conv(0, middle - 2)
    recv(has_l, [parts[3]])
    correlate(middle + 2, middle - 2)
    first_conv(middle, rows + 2 - middle)
    second_conv(middle - 2, rows + 2 - middle)

    sent(has_r, small_r + parts)
    sent(has_l, small_l)
    sent(has_d, down + down_edges)
    sent(has_u, up + up_edges)

    @pl.loop(0, rows)
    def _(h):
        out_copy(h).wait()


def vol_cols(width):
    return -(-(width + 2 * G) // TILE) * TILE


def TILE_WINDOW(disp):
    return -(-(TILE + disp - 1) // LANES) * LANES


def local(ncol, nrow, left, right, w1, w2):
    rows, width, chans = left.shape
    disp = w1.shape[2]
    outs = w1.shape[3]
    w1 = w1.reshape(-1, outs)
    w2 = w2.reshape(-1, outs)
    span = vol_cols(width) - TILE + TILE_WINDOW(disp)
    hbm = pl.BlockSpec(memory_space=pl.ANY)
    copies = 19
    return pl.pallas_call(
        functools.partial(fixed, ncol, nrow),
        out_shape=jax.ShapeDtypeStruct((rows, width, outs), BF16),
        in_specs=[hbm] * 4,
        out_specs=hbm,
        scratch_shapes=[
            pltpu.VMEM((rows + 4, span, chans), BF16),
            pltpu.VMEM((rows + 4, vol_cols(width), chans), BF16),
            pltpu.VMEM((span, chans), BF16),
            pltpu.VMEM((rows + 4, vol_cols(width) + G, 3 * disp), BF16),
            pltpu.VMEM((rows + 2, width + 3 * G, 3 * outs), BF16),
            pltpu.VMEM(w1.shape, BF16),
            pltpu.VMEM(w2.shape, BF16),
            pltpu.VMEM((rows, width, outs), BF16),
            pltpu.SemaphoreType.DMA((4,)),
            pltpu.SemaphoreType.DMA((rows,)),
            pltpu.SemaphoreType.DMA((copies,)),
            pltpu.SemaphoreType.DMA((copies,)),
        ],
        compiler_params=pltpu.CompilerParams(
            collective_id=0, has_side_effects=True, vmem_limit_bytes=60 * 1024 * 1024
        ),
    )(left, right, w1, w2)


def fixed(ncol, nrow, *refs):
    kernel(ncol, nrow, *refs)


def solution(mesh):
    in_specs = (P(("strip", "row"), "col", None), P(("strip", "row"), "col", None), P(), P())
    out_specs = P(("strip", "row"), "col", None)
    return jax.shard_map(
        functools.partial(local, mesh.shape["col"], mesh.shape["row"]),
        mesh=mesh, in_specs=in_specs, out_specs=out_specs, check_vma=False,
    )
```

time: 147 us -> 38 us (0.26)
  local copies, waits for them, and re-layouts: 72.5 us -> 3.05 us
  Pallas kernels: 0 us -> 34.8 us
  starting transfers between devices: 27.8 us -> 0 us
  waiting for transfers between devices: 25 us -> 0 us
  matrix products: 14 us -> 0 us
  other arithmetic: 6.12 us -> 0 us
    pallas_call x0 -> x1, Pallas kernels: none -> 34.8 us  [local(): pl.pallas_call(functools.partial(fixed, ncol, nrow), out_shape=jax.ShapeD...]
    ppermute x9 -> x0, starting transfers between devices: 27.8 us -> none  [the longest x4 17.1 us: extended_2(): lax.ppermute(lax.slice_in_dim(block, block.shape[dim] - width, None, axis...]
    ppermute x9 -> x0, waiting for transfers between devices: 25 us -> none  [the longest x4 12.4 us: extended_2(): lax.ppermute(lax.slice_in_dim(block, 0, width, axis=dim), axis, backward)]
    rev x1 -> x0, local copies, waits for them, and re-layouts: 22.5 us -> none  [correlate(): banded = skewed[..., 1:disparities + 1][..., ::-1]]
    reshape x2 -> x0, local copies, waits for them, and re-layouts: 18.2 us -> none  [the longest x1 13.3 us: correlate(): flat_scores.reshape(row_count, block_count, disparities, 2 * disparities...]
    conv_general_dilated x2 -> x0, matrix products: 10.8 us -> none  [convolve_valid(): lax.conv_general_dilated(padded[None], kernel, (1, 1), 'VALID', dimension...]
    conv_general_dilated x5 -> x0, local copies, waits for them, and re-layouts: 8.56 us -> none  [convolve_valid(): lax.conv_general_dilated(padded[None], kernel, (1, 1), 'VALID', dimension...]
    mul x1 -> x0, local copies, waits for them, and re-layouts: 6.22 us -> none  [correlate(): scores = scores * (1.0 / jnp.sqrt(jnp.float32(chan_count)))]
  transfers between devices with their start and end apart: 9 -> 0, of which waited for: 7 -> 0; matrix products, arithmetic and copies ran while one was open for 0% -> 0% of each run, Pallas kernels for 0% -> 0%
where the time goes in v1:
time: 38 us; the launch traced here: 37.9 us
  Pallas kernels  34.8 us (92%)
  local copies, waits for them, and re-layouts  3.05 us (8%)
    pallas_call x1, Pallas kernels, local(): pl.pallas_call(functools.partial(fixed, ncol, nrow), out_shape=jax.ShapeD...  34.8 us
    unnamed x1, local copies, waits for them, and re-layouts  3.05 us

profile of v1, /device:TPU:1, one launch (start us, length us, event | category | flops | bytes accessed | tf_op | source)
XLA Modules:
  0.0 37.9 jit_solution(16926507181383782055)
XLA Ops:
  0.0 34.8 %shard_map.46 = bf16[8,512,256]{2,1,0:T(8,128)(2,1)} custom-call(bf16[8,512,128]{2,1,0:T(8,128)(2,1)} %refs_0_.1, bf16[8,512,128]{2,1,0:T(8,128)(2,1)} %refs_1_.1, bf16[2304,256]{1,0:T(8,128)(2,1)} %bitcast.2, bf16[2304,256]{1,0:T(8,128)(2,1)} %bitcast.3), custom_call_target="tpu_custom_call" | custom-call | tf_op jit(solution)/shard_map/pallas_call | solution.py:234
  34.8 3.0 %copy.6 = bf16[8,512,256]{2,1,0:T(8,128)(2,1)} copy(bf16[8,512,256]{2,1,0:T(8,128)(2,1)} %shard_map.46) | data formatting | bytes 4194304

commit v2 on v1

--- a/solution.py
+++ b/solution.py
@@ -17,7 +17,7 @@
 
 def kernel(
     ncol, nrow, left, right, w1_hbm, w2_hbm, out,
-    rext, lext, rrev, vol3, hid3, w1, w2, obuf, lsem, osem, ssem, rsem,
+    rext, lext, rrev, vol3, hid3, w1, w2, lsem, ssem, rsem,
 ):
     rows, width, chans = left.shape
     disp = w1_hbm.shape[0] // 9
@@ -33,14 +33,6 @@
     window = TILE_WINDOW(disp)
     hcols = width + G
 
-    rext[:, 0:reach] = jnp.zeros((rows + 4, reach, chans), BF16)
-    rext[:, reach + width :] = jnp.zeros((rows + 4, span - reach - width, chans), BF16)
-    lext[:, 0:G] = jnp.zeros((rows + 4, G, chans), BF16)
-    lext[:, G + width :] = jnp.zeros((rows + 4, lext.shape[1] - G - width, chans), BF16)
-    for ref, at in ((rext, reach), (lext, G)):
-        ref[0:2, at : at + width] = jnp.zeros((2, width, chans), BF16)
-        ref[rows + 2 :, at : at + width] = jnp.zeros((2, width, chans), BF16)
-
     own = [
         pltpu.make_async_copy(right, rext.at[2 : rows + 2, reach : reach + width], lsem.at[0]),
         pltpu.make_async_copy(left, lext.at[2 : rows + 2, G : G + width], lsem.at[1]),
@@ -49,6 +41,33 @@
     ]
     for copy in own:
         copy.start()
+
+    edge = reach + width
+    rext[:, edge + G :] = jnp.zeros((rows + 4, span - edge - G, chans), BF16)
+    lext[:, 2 * G + width :] = jnp.zeros((rows + 4, lext.shape[1] - 2 * G - width, chans), BF16)
+
+    def clear(ref, *at):
+        ref[at] = jnp.zeros(ref.at[at].shape, BF16)
+
+    @pl.when(jnp.logical_not(has_l))
+    def _():
+        clear(rext, slice(0, rows + 4), slice(0, reach))
+        clear(lext, slice(0, rows + 4), slice(0, G))
+
+    @pl.when(jnp.logical_not(has_r))
+    def _():
+        clear(rext, slice(0, rows + 4), slice(edge, edge + G))
+        clear(lext, slice(0, rows + 4), slice(G + width, 2 * G + width))
+
+    @pl.when(jnp.logical_not(has_u))
+    def _():
+        clear(rext, slice(0, 2), slice(0, edge + G))
+        clear(lext, slice(0, 2), slice(0, 2 * G + width))
+
+    @pl.when(jnp.logical_not(has_d))
+    def _():
+        clear(rext, slice(rows + 2, rows + 4), slice(0, edge + G))
+        clear(lext, slice(rows + 2, rows + 4), slice(0, 2 * G + width))
 
     barrier = pltpu.get_barrier_semaphore()
     for has, to in ((has_l, to_l), (has_r, to_r), (has_u, to_u), (has_d, to_d)):
@@ -126,92 +145,125 @@
     start(has_d, down)
     start(has_u, up)
 
-    block = span // 4
-    i = lax.broadcasted_iota(jnp.int32, (block, block), 0)
-    j = lax.broadcasted_iota(jnp.int32, (block, block), 1)
-    flip = jnp.where(i + j == block - 1, 1.0, 0.0).astype(BF16)
     scale = 1.0 / jnp.sqrt(F32(chans))
-
-    def correlate(first, count):
-        @pl.loop(first, first + count)
-        def _(r):
-            for q in range(4):
-                piece = jnp.dot(
-                    flip, rext[r, q * block : (q + 1) * block, :], preferred_element_type=F32
-                )
-                rrev[(3 - q) * block : (4 - q) * block, :] = piece.astype(BF16)
-            for t in range(tiles):
+    cut = -(-reach // TILE)
+    fresh = -(-(span - TILE * cut) // (2 * G)) * (2 * G)
+
+    def flip(size):
+        i = lax.broadcasted_iota(jnp.int32, (size, size), 0)
+        j = lax.broadcasted_iota(jnp.int32, (size, size), 1)
+        return jnp.where(i + j == size - 1, 1.0, 0.0).astype(BF16)
+
+    def correlate(first, count, right_part):
+        size = fresh // 2 if right_part else (span - fresh) // 2
+        base = 0 if right_part else fresh
+
+        @pl.loop(0, count // 2)
+        def _(p):
+            pair = [first + 2 * p, first + 2 * p + 1]
+            turn = flip(size)
+            for q in range(2):
+                for r in pair:
+                    high = span - base - q * size
+                    piece = jnp.dot(turn, rext[r, high - size : high, :], preferred_element_type=F32)
+                    rrev[r, base + q * size : base + (q + 1) * size, :] = piece.astype(BF16)
+            for t in range(cut, tiles) if right_part else range(cut):
                 at = span - window - TILE * t
-                scores = lax.dot_general(
-                    lext[r, TILE * t : TILE * (t + 1), :],
-                    rrev[at : at + window, :],
-                    (((1,), (1,)), ((), ())),
-                    preferred_element_type=F32,
-                )
-                turned = pltpu.roll(
-                    scores, disp + 1, 1, stride=1, stride_axis=0
-                )[:, :disp]
-                value = (turned * scale).astype(BF16)
+                for r in pair:
+                    scores = lax.dot_general(
+                        lext[r, TILE * t : TILE * (t + 1), :],
+                        rrev[r, at : at + window, :],
+                        (((1,), (1,)), ((), ())),
+                        preferred_element_type=F32,
+                    )
+                    turned = pltpu.roll(
+                        scores, window - TILE_SHIFT(disp), 1, stride=1, stride_axis=0
+                    )[:, :disp]
+                    value = (turned * scale).astype(BF16)
+                    for b in range(3):
+                        vol3[r, TILE * t + 2 - b : TILE * (t + 1) + 2 - b, b * disp : (b + 1) * disp] = value
+
+    bar = -(-(TILE * cut + 2) // G) * G
+
+    def first_conv(first, count, right_part):
+        low, high = (bar, G + hcols) if right_part else (G, bar)
+        size = high - low
+
+        @pl.loop(0, count // 2)
+        def _(p):
+            g = first + 2 * p
+            x = jnp.concatenate(
+                [vol3[pl.ds(g + a, 2), low:high, :].reshape(2 * size, 3 * disp) for a in range(3)], axis=1
+            )
+            acc = jnp.dot(x, w1[...], preferred_element_type=F32)
+            j = lax.broadcasted_iota(jnp.int32, (size, 1), 0)
+            at_col = col * width + j + (low - G - 1)
+            inside_col = (at_col >= 0) & (at_col < ncol * width)
+            for k in range(2):
+                at_row = row * rows + g + k - 1
+                inside = inside_col & (at_row >= 0) & (at_row < nrow * rows)
+                value = jnp.maximum(acc[k * size : (k + 1) * size], 0.0)
+                value = jnp.where(inside, value, 0.0).astype(BF16)
                 for b in range(3):
-                    vol3[r, TILE * t + 2 - b : TILE * (t + 1) + 2 - b, b * disp : (b + 1) * disp] = value
-
-    def first_conv(first, count):
-        @pl.loop(first, first + count)
-        def _(g):
-            x = jnp.concatenate([vol3[g + a, G : G + hcols, :] for a in range(3)], axis=1)
-            acc = jnp.dot(x, w1[...], preferred_element_type=F32)
-            j = lax.broadcasted_iota(jnp.int32, (hcols, 1), 0)
-            at_row = row * rows + g - 1
-            at_col = col * width + j - 1
-            inside = (at_col >= 0) & (at_col < ncol * width) & (at_row >= 0) & (at_row < nrow * rows)
-            value = jnp.where(inside, jnp.maximum(acc, 0.0), 0.0).astype(BF16)
-            for b in range(3):
-                hid3[g, G - b : G - b + hcols, b * disp : (b + 1) * disp] = value
-
-    def out_copy(h):
-        return pltpu.make_async_copy(obuf.at[h], out.at[h], osem.at[h])
-
-    def second_conv(first, count):
-        @pl.loop(first, first + count)
-        def _(h):
-            x = jnp.concatenate([hid3[h + a, G : G + width, :] for a in range(3)], axis=1)
+                    hid3[g + k, low - b : high - b, b * disp : (b + 1) * disp] = value
+
+    def second_conv(first, count, right_part):
+        low, high = (bar, G + width) if right_part else (G, bar)
+        size = high - low
+
+        @pl.loop(0, count // 2)
+        def _(p):
+            h = first + 2 * p
+            x = jnp.concatenate(
+                [hid3[pl.ds(h + a, 2), low:high, :].reshape(2 * size, 3 * disp) for a in range(3)], axis=1
+            )
             acc = jnp.dot(x, w2[...], preferred_element_type=F32)
-            obuf[h] = jnp.maximum(acc, 0.0).astype(BF16)
-            out_copy(h).start()
-
+            out[pl.ds(h, 2), low - G : high - G] = jnp.maximum(acc, 0.0).astype(BF16).reshape(2, size, disp)
+
+    RIGHT, LEFT = True, False
     own[0].wait()
     own[1].wait()
-    recv(has_l, small_r)
     recv(has_r, small_l)
-    recv(has_l, [parts[0]])
+    correlate(2, rows, RIGHT)
+    recv(has_l, small_r + [parts[0]])
     start(has_u, up_edges)
-    correlate(2, 2)
+    own[2].wait()
+    first_conv(2, rows - 2, RIGHT)
+    own[3].wait()
+    second_conv(2, rows - 4, RIGHT)
+    correlate(2, 2, LEFT)
     recv(has_l, [parts[1]])
     start(has_d, down_edges)
-    correlate(rows, 2)
+    correlate(rows, 2, LEFT)
     recv(has_d, up + up_edges)
-    correlate(rows + 2, 2)
+    correlate(rows + 2, 2, RIGHT)
+    correlate(rows + 2, 2, LEFT)
+    first_conv(rows, 2, RIGHT)
+    first_conv(rows, 2, LEFT)
+    second_conv(rows - 2, 2, RIGHT)
     recv(has_l, [parts[2]])
-    correlate(4, middle - 2)
-    own[2].wait()
-    own[3].wait()
+    correlate(4, middle - 2, LEFT)
+    first_conv(2, middle - 2, LEFT)
     recv(has_u, down + down_edges)
-    correlate(0, 2)
-    first_conv(0, middle)
-    second_conv(0, middle - 2)
+    correlate(0, 2, RIGHT)
+    correlate(0, 2, LEFT)
+    first_conv(0, 2, RIGHT)
+    first_conv(0, 2, LEFT)
+    second_conv(0, 2, RIGHT)
+    second_conv(0, middle - 2, LEFT)
     recv(has_l, [parts[3]])
-    correlate(middle + 2, middle - 2)
-    first_conv(middle, rows + 2 - middle)
-    second_conv(middle - 2, rows + 2 - middle)
+    correlate(middle + 2, rows - 2 - middle, LEFT)
+    first_conv(middle, rows - middle, LEFT)
+    second_conv(middle - 2, rows + 2 - middle, LEFT)
 
     sent(has_r, small_r + parts)
     sent(has_l, small_l)
     sent(has_d, down + down_edges)
     sent(has_u, up + up_edges)
 
-    @pl.loop(0, rows)
-    def _(h):
-        out_copy(h).wait()
+
+def TILE_SHIFT(disp):
+    return TILE_WINDOW(disp) - disp - 1
 
 
 def vol_cols(width):
@@ -233,25 +285,23 @@
     copies = 19
     return pl.pallas_call(
         functools.partial(fixed, ncol, nrow),
-        out_shape=jax.ShapeDtypeStruct((rows, width, outs), BF16),
+        out_shape=pltpu.VMEM((rows, width, outs), BF16),
         in_specs=[hbm] * 4,
-        out_specs=hbm,
+        out_specs=pl.BlockSpec(memory_space=pltpu.VMEM),
         scratch_shapes=[
             pltpu.VMEM((rows + 4, span, chans), BF16),
             pltpu.VMEM((rows + 4, vol_cols(width), chans), BF16),
-            pltpu.VMEM((span, chans), BF16),
+            pltpu.VMEM((rows + 4, span, chans), BF16),
             pltpu.VMEM((rows + 4, vol_cols(width) + G, 3 * disp), BF16),
             pltpu.VMEM((rows + 2, width + 3 * G, 3 * outs), BF16),
             pltpu.VMEM(w1.shape, BF16),
             pltpu.VMEM(w2.shape, BF16),
-            pltpu.VMEM((rows, width, outs), BF16),
             pltpu.SemaphoreType.DMA((4,)),
-            pltpu.SemaphoreType.DMA((rows,)),
             pltpu.SemaphoreType.DMA((copies,)),
             pltpu.SemaphoreType.DMA((copies,)),
         ],
         compiler_params=pltpu.CompilerParams(
-            collective_id=0, has_side_effects=True, vmem_limit_bytes=60 * 1024 * 1024
+            collective_id=0, has_side_effects=True, vmem_limit_bytes=67_043_328 - 2 * rows * width * outs - 2**18
         ),
     )(left, right, w1, w2)
 

time: 38 us -> 32.5 us (0.86)
  the two profiles are of different devices: /device:TPU:1 before, /device:TPU:0 now
where the time goes in v2:
time: 32.5 us; the launch traced here: 32.3 us
  Pallas kernels  31 us (95%)
  local copies, waits for them, and re-layouts  1.32 us (4%)
    pallas_call x1, Pallas kernels, local(): pl.pallas_call(functools.partial(fixed, ncol, nrow), out_shape=pltpu.VMEM...  31 us
    unnamed x1, local copies, waits for them, and re-layouts  1.32 us

profile of v2, /device:TPU:0, one launch (start us, length us, event | category | flops | bytes accessed | tf_op | source)
XLA Modules:
  0.0 32.3 jit_solution(13837900916153224544)
XLA Ops:
  0.0 31.0 %shard_map.46 = bf16[8,512,256]{2,1,0:T(8,128)(2,1)S(1)} custom-call(bf16[8,512,128]{2,1,0:T(8,128)(2,1)} %refs_0_.1, bf16[8,512,128]{2,1,0:T(8,128)(2,1)} %refs_1_.1, bf16[2304,256]{1,0:T(8,128)(2,1)} %bitcast.2, bf16[2304,256]{1,0:T(8,128)(2,1)} %bitcast.3), custom_call_target="tpu_custom_call" | custom-call | tf_op jit(solution)/shard_map/pallas_call | solution.py:286
  31.0 1.3 %copy.6 = bf16[8,512,256]{2,1,0:T(8,128)(2,1)} copy(bf16[8,512,256]{2,1,0:T(8,128)(2,1)S(1)} %shard_map.46) | data formatting | bytes 4194304
